TPU v7x, 256 devices: a whole 4x4x8 slice. The times are simulated.
256 devices in a mesh: cube: 64 (over z, y, core), pair: 4 (over x).
Axes of the slice: x: 4, y: 4, z: 8, core: 2. Of those that a mesh axis runs over, the one named last changes fastest.
Arguments:
- own_partial: float32 [3, 16384, 512], P(None, 'cube'), may hold values from -6 to 6
- spill_partial: float32 [3, 16384, 512], P(None, 'cube'), may hold values from -6 to 6
- spill_box: int32 [16384], P('cube'), may hold values from 0 to 255, as said below
- sources: int32 [16384, 189], P('cube'), may hold values from 0 to 16383, as said below
- reflections: int32 [16384, 189], P('cube'), may hold values from 0 to 15
- operators: bfloat16 [16, 512, 512], P('pair'), may hold values from -0.01953125 to 0.01953125
Outputs:
- local_own: float32 [3, 16384, 512], P(None, 'cube', 'pair')
- local_spill: float32 [3, 16384, 512], P(None, 'cube', 'pair')
Inputs may be any that keep to these rules, and one draw needn't show every extreme that they name: The sources of box b lie on b's owner or on the owner just before or after it: from max(0, (b // 256 - 1) * 256) to min(16384, (b // 256 + 2) * 256) - 1. A source may repeat within a list. `spill_box`: the 64 entries of each aligned run of 64 are distinct.
All inputs are finite; a program needn't handle non-finite values.
Results may differ from a plain program's by a relative error of at most 0.0095.
Values may be sent and summed in bfloat16 or wider, within the bound.
No kernel may reach another device: no remote copies, remote signals or barrier semaphores. Data moves between devices by JAX's collectives and lax.ppermute only.
A program may use at most 64 MiB of HBM per device.

v0:
```python
import jax
import jax.numpy as jnp
from jax import lax
from jax.sharding import PartitionSpec as P

SPILL = 2


def passed_along(value, axis, steps):
    count = lax.axis_size(axis)
    first, last = (max(0, -steps), min(count, count - steps))
    return lax.ppermute(value, axis, [(source, source + steps) for source in range(first, last)])


def padded(block, sides, width):
    for axis, dim in sides:
        count = lax.axis_size(axis)
        forward = [(i, i + 1) for i in range(count - 1)]
        backward = [(target, source) for source, target in forward]
        low = lax.ppermute(
            lax.slice_in_dim(block, block.shape[dim] - width, None, axis=dim), axis, forward
        )
        high = lax.ppermute(lax.slice_in_dim(block, 0, width, axis=dim), axis, backward)
        block = jnp.concatenate([low, block, high], axis=dim)
    return block


def spill_offsets():
    return [shift_by for shift_by in range(-SPILL, SPILL + 1) if shift_by != 0]


def split_pair(values):
    upper = values.astype(jnp.bfloat16)
    lower = (values - upper.astype(jnp.float32)).astype(jnp.bfloat16)
    return (upper, lower)


def split_einsum(form, exact_side, data_side):
    upper, lower = split_pair(data_side)
    first = jnp.einsum(form, exact_side, upper, preferred_element_type=jnp.float32)
    return first + jnp.einsum(form, exact_side, lower, preferred_element_type=jnp.float32)


def count_table(src_local, rel_refl, groups, extent):
    column_total = groups * extent
    low_width = 128
    high_width = (column_total + low_width - 1) // low_width
    inside = (rel_refl >= 0) & (rel_refl < groups)
    keyed = jnp.where(inside, rel_refl * extent + src_local, -1)
    high_part = jnp.where(inside, keyed // low_width, -1)
    low_part = jnp.where(inside, keyed % low_width, 0)
    high_ids = jnp.arange(high_width, dtype=jnp.int32)
    low_ids = jnp.arange(low_width, dtype=jnp.int32)
    high_onehot = (high_part[:, :, None] == high_ids).astype(jnp.bfloat16)
    low_onehot = (low_part[:, :, None] == low_ids).astype(jnp.bfloat16)
    counter = jnp.einsum(
        "tjh,tjl->thl", high_onehot, low_onehot, preferred_element_type=jnp.float32
    )
    counter = counter.reshape(keyed.shape[0], high_width * low_width)
    return counter.astype(jnp.bfloat16)


def add_reflection(summed, counter, position, window, operator, reflection):
    extent = window.shape[1]
    counts = lax.dynamic_slice_in_dim(counter, position * extent, extent, 1)
    bit_ids = jnp.arange(3, dtype=jnp.int32)
    sign_factor = (1 - 2 * (jnp.right_shift(reflection, bit_ids) & 1)).astype(jnp.float32)[
        :, None, None
    ]
    applied_all = jnp.einsum("cse,ef->csf", window, operator, preferred_element_type=jnp.float32)
    applied = split_einsum("ts,csf->ctf", counts, applied_all)
    return summed + sign_factor * applied


def on_device(own_partial, spill_partial, spill_box, sources, reflections, operators):
    box_count = own_partial.shape[1]
    coeff_count = operators.shape[2]
    slot_count = spill_box.shape[0] // (2 * SPILL)
    cube_index = lax.axis_index("cube")
    multipole = own_partial
    selectors = []
    box_ids = jnp.arange(box_count, dtype=jnp.int32)[None, :]
    for group_id, offset in enumerate(spill_offsets()):
        outgoing = spill_partial[:, group_id * slot_count : (group_id + 1) * slot_count]
        labels = spill_box[group_id * slot_count : (group_id + 1) * slot_count].astype(jnp.float32)
        got_part, got_labels = passed_along((outgoing, labels), "cube", offset)
        picker = (got_labels.astype(jnp.int32)[:, None] == box_ids).astype(jnp.bfloat16)
        multipole = multipole + split_einsum("sb,cse->cbe", picker, got_part)
        selectors.append(picker)
    window = padded(multipole.astype(jnp.bfloat16), (("cube", 1),), box_count)
    extent = window.shape[1]
    src_local = sources - (cube_index - 1) * box_count
    held_count = operators.shape[0]
    leading = lax.axis_index("pair") * held_count
    counter = count_table(src_local, reflections - leading, held_count, extent)
    summed = jnp.zeros((3, box_count, coeff_count), jnp.float32)
    for position in range(held_count):
        summed = add_reflection(
            summed, counter, position, window, operators[position], leading + position
        )
    local_field = lax.psum_scatter(summed, "pair", scatter_dimension=2, tiled=True)
    returned = []
    for group_id, offset in enumerate(spill_offsets()):
        picked = split_einsum("sb,cbe->cse", selectors[group_id], local_field)
        returned.append(passed_along(picked, "cube", -offset))
    return (local_field, jnp.concatenate(returned, axis=1))


def solution(mesh):
    in_specs = (
        P(None, "cube", None),
        P(None, "cube", None),
        P("cube"),
        P("cube", None),
        P("cube", None),
        P("pair", None, None),
    )
    out_specs = (P(None, "cube", "pair"), P(None, "cube", "pair"))
    return jax.shard_map(
        on_device, mesh=mesh, in_specs=in_specs, out_specs=out_specs, check_vma=False
    )
```

profile of v0, /device:TPU:120, one launch (start us, length us, event | category | flops | bytes accessed | tf_op | source)
XLA Modules:
  0.0 152.1 jit_solution(12556728221196462873)
XLA Ops:
  7.2 2.4 %fusion.99 = (f32[3,64,512]{2,1,0:T(8,128)S(1)}, f32[3,64,512]{2,1,0:T(8,128)S(1)}, f32[3,64,512]{2,1,0:T(8,128)S(1)}, f32[3,64,512]{2,1,0:T(8,128)}) fusion(f32[3,256,512]{2,1,0:T(8,128)} %param.7), kind=kLoop, calls=%fused_computation.130 | loop fusion | bytes 3145728 | tf_op jit(solution)/shard_map/slice | solution.py:84
  9.6 1.9 %collective-permute-start.5 = (f32[3,64,512]{2,1,0:T(8,128)}, f32[3,64,512]{2,1,0:T(8,128)S(1)}, u32[]{:S(2)}, u32[]{:S(2)}) collective-permute-start(f32[3,64,512]{2,1,0:T(8,128)} %get-tuple-element.9), channel_id=1, source_target_pairs={{0,4},{4,8},{8,12},{12,16},{16,20},{20,24},{24,28},{28,32},{32,36}... | collective-permute-start | bytes 1179656 | tf_op jit(solution)/shard_map/ppermute | solution.py:12
  11.6 2.6 %collective-permute-start = (f32[64]{0:T(128)S(1)}, f32[64]{0:T(128)S(1)}, u32[]{:S(2)}, u32[]{:S(2)}) collective-permute-start(f32[64]{0:T(128)S(1)} %get-tuple-element.12), channel_id=1, source_target_pairs={{8,0},{12,4},{16,8},{20,12},{24,16},{28,20},{32,24},{36,28},{40,32... | collective-permute-start | bytes 776 | tf_op jit(solution)/shard_map/ppermute | solution.py:12
  14.3 2.4 %collective-permute-start.1 = (f32[3,64,512]{2,1,0:T(8,128)S(1)}, f32[3,64,512]{2,1,0:T(8,128)S(1)}, u32[]{:S(2)}, u32[]{:S(2)}) collective-permute-start(f32[3,64,512]{2,1,0:T(8,128)S(1)} %get-tuple-element.6), channel_id=1, source_target_pairs={{8,0},{12,4},{16,8},{20,12},{24,16},{28,20},{32,24},{36,28},{40,32... | collective-permute-start | bytes 1179656 | tf_op jit(solution)/shard_map/ppermute | solution.py:12
  16.7 3.1 %collective-permute-start.2 = (f32[64]{0:T(128)S(1)}, f32[64]{0:T(128)S(1)}, u32[]{:S(2)}, u32[]{:S(2)}) collective-permute-start(f32[64]{0:T(128)S(1)} %get-tuple-element.13), channel_id=1, source_target_pairs={{4,0},{8,4},{12,8},{16,12},{20,16},{24,20},{28,24},{32,28},{36,32}... | collective-permute-start | bytes 776 | tf_op jit(solution)/shard_map/ppermute | solution.py:12
  19.7 1.9 %collective-permute-start.3 = (f32[3,64,512]{2,1,0:T(8,128)S(1)}, f32[3,64,512]{2,1,0:T(8,128)S(1)}, u32[]{:S(2)}, u32[]{:S(2)}) collective-permute-start(f32[3,64,512]{2,1,0:T(8,128)S(1)} %get-tuple-element.7), channel_id=1, source_target_pairs={{4,0},{8,4},{12,8},{16,12},{20,16},{24,20},{28,24},{32,28},{36,32}... | collective-permute-start | bytes 1179656 | tf_op jit(solution)/shard_map/ppermute | solution.py:12
  21.7 0.2 fusion.40
  22.1 2.5 %collective-permute-start.4 = (f32[64]{0:T(128)S(1)}, f32[64]{0:T(128)S(1)}, u32[]{:S(2)}, u32[]{:S(2)}) collective-permute-start(f32[64]{0:T(128)S(1)} %get-tuple-element.15), channel_id=1, source_target_pairs={{0,4},{4,8},{8,12},{12,16},{16,20},{20,24},{24,28},{28,32},{32,36}... | collective-permute-start | bytes 776 | tf_op jit(solution)/shard_map/ppermute | solution.py:12
  24.6 0.6 collective-permute-done.2
  25.1 6.8 %collective-permute-start.6 = (f32[64]{0:T(128)S(1)}, f32[64]{0:T(128)S(1)}, u32[]{:S(2)}, u32[]{:S(2)}) collective-permute-start(f32[64]{0:T(128)S(1)} %get-tuple-element.14), channel_id=1, source_target_pairs={{0,8},{4,12},{8,16},{12,20},{16,24},{20,28},{24,32},{28,36},{32,40... | collective-permute-start | bytes 776 | tf_op jit(solution)/shard_map/ppermute | solution.py:12
  32.0 5.7 %collective-permute-start.7 = (f32[3,64,512]{2,1,0:T(8,128)S(1)}, f32[3,64,512]{2,1,0:T(8,128)S(1)}, u32[]{:S(2)}, u32[]{:S(2)}) collective-permute-start(f32[3,64,512]{2,1,0:T(8,128)S(1)} %get-tuple-element.8), channel_id=1, source_target_pairs={{0,8},{4,12},{8,16},{12,20},{16,24},{20,28},{24,32},{28,36},{32,40... | collective-permute-start | bytes 1179656 | tf_op jit(solution)/shard_map/ppermute | solution.py:12
  37.7 0.5 fusion.44
  38.2 0.5 fusion.51
  38.7 0.5 fusion.43
  39.2 0.5 fusion.54
  39.7 0.5 fusion.42
  40.1 0.5 fusion.57
  40.6 5.1 %collective-permute-done.7 = f32[3,64,512]{2,1,0:T(8,128)S(1)} collective-permute-done((f32[3,64,512]{2,1,0:T(8,128)S(1)}, f32[3,64,512]{2,1,0:T(8,128)S(1)}, u32[]{:S(2)}, u32[]{:S(2)}) %collective-permute-start.7) | collective-permute-done | bytes 393248 | tf_op jit(solution)/shard_map/ppermute | solution.py:12
  45.7 0.5 fusion.48
  46.2 1.3 fusion.9
  47.5 2.0 %collective-permute-start.8 = (bf16[3,256,512]{2,1,0:T(8,128)(2,1)S(1)}, bf16[3,256,512]{2,1,0:T(8,128)(2,1)}, u32[]{:S(2)}, u32[]{:S(2)}) collective-permute-start(bf16[3,256,512]{2,1,0:T(8,128)(2,1)S(1)} %fusion.9), channel_id=1, source_target_pairs={{0,4},{4,8},{8,12},{12,16},{16,20},{20,24},{24,28},{28,32},{32,36}... | collective-permute-start | bytes 2359304 | tf_op jit(solution)/shard_map/ppermute | solution.py:20
  49.5 3.5 %collective-permute-start.9 = (bf16[3,256,512]{2,1,0:T(8,128)(2,1)S(1)}, bf16[3,256,512]{2,1,0:T(8,128)(2,1)}, u32[]{:S(2)}, u32[]{:S(2)}) collective-permute-start(bf16[3,256,512]{2,1,0:T(8,128)(2,1)S(1)} %fusion.9), channel_id=1, source_target_pairs={{4,0},{8,4},{12,8},{16,12},{20,16},{24,20},{28,24},{32,28},{36,32}... | collective-permute-start | bytes 2359304 | tf_op jit(solution)/shard_map/ppermute | solution.py:23
  53.1 0.9 iota_compare_fusion.18
  54.1 12.9 %fusion.7 = bf16[256,24,128]{2,1,0:T(8,128)(2,1)S(1)} fusion(s32[256,189]{1,0:T(8,128)S(1)} %copy.9, pred[256,189,24]{1,2,0:T(8,128)(4,1)S(1)} %iota_compare_fusion.18), kind=kOutput, calls=%fused_computation.14 | convolution fusion | flops 304250880 | bytes 2927616 | tf_op jit(solution)/shard_map/tjh,tjl->thl/dot_general | solution.py:56
  67.0 0.3 copy.45
  67.4 2.9 %fusion.34 = f32[3,768,512]{2,1,0:T(8,128)S(1)} fusion(bf16[4,512,512]{2,1,0:T(8,128)(2,1)} %param.11, bf16[3,256,512]{2,1,0:T(8,128)(2,1)} %collective-permute-done.9, bf16[3,256,512]{2,1,0:T(8,128)(2,1)S(1)} %fusion.9, bf16[3,256,512]{2,1,0:T(8,128)(2,1)} %collective-permute-done.8), kind=kOutput, calls=%fused_computation.51 | convolution fusion | flops 1215037440 | bytes 7602176 | tf_op jit(solution)/shard_map/cse,ef->csf/dot_general | solution.py:70
  70.3 0.9 fusion.3
  71.2 0.9 fusion.22
  72.1 0.7 copy-done.5
  72.8 2.8 %fusion.32 = f32[3,768,512]{2,1,0:T(8,128)S(1)} fusion(bf16[4,512,512]{2,1,0:T(8,128)(2,1)S(1)} %copy-done.5, bf16[3,256,512]{2,1,0:T(8,128)(2,1)} %collective-permute-done.9, bf16[3,256,512]{2,1,0:T(8,128)(2,1)S(1)} %fusion.9, bf16[3,256,512]{2,1,0:T(8,128)(2,1)} %collective-permute-done.8), kind=kOutput, calls=%fused_computation.49 | convolution fusion | flops 1215037440 | bytes 7602176 | tf_op jit(solution)/shard_map/cse,ef->csf/dot_general | solution.py:70
  75.6 0.9 fusion.4
  76.5 0.9 fusion.19
  77.3 2.8 %fusion.30 = f32[3,768,512]{2,1,0:T(8,128)S(1)} fusion(bf16[4,512,512]{2,1,0:T(8,128)(2,1)S(1)} %copy-done.5, bf16[3,256,512]{2,1,0:T(8,128)(2,1)} %collective-permute-done.9, bf16[3,256,512]{2,1,0:T(8,128)(2,1)S(1)} %fusion.9, bf16[3,256,512]{2,1,0:T(8,128)(2,1)} %collective-permute-done.8), kind=kOutput, calls=%fused_computation.47 | convolution fusion | flops 1215037440 | bytes 7602176 | tf_op jit(solution)/shard_map/cse,ef->csf/dot_general | solution.py:70
  80.1 0.9 fusion.5
  81.0 0.9 fusion.16
  81.9 2.8 %fusion.28 = f32[3,768,512]{2,1,0:T(8,128)S(1)} fusion(bf16[4,512,512]{2,1,0:T(8,128)(2,1)S(1)} %copy-done.5, bf16[3,256,512]{2,1,0:T(8,128)(2,1)} %collective-permute-done.9, bf16[3,256,512]{2,1,0:T(8,128)(2,1)S(1)} %fusion.9, bf16[3,256,512]{2,1,0:T(8,128)(2,1)} %collective-permute-done.8), kind=kOutput, calls=%fused_computation.45 | convolution fusion | flops 1215037440 | bytes 7602176 | tf_op jit(solution)/shard_map/cse,ef->csf/dot_general | solution.py:70
  84.7 0.8 fusion.6
  85.5 2.9 %add_bitcast_fusion = f32[3,256,512]{1,2,0:T(8,128)} fusion(f32[3,512,256]{2,1,0:T(8,128)S(1)} %fusion.6, f32[3,512,256]{2,1,0:T(8,128)S(1)} %fusion.16, f32[3,512,256]{2,1,0:T(8,128)S(1)} %fusion.5, f32[3,512,256]{2,1,0:T(8,128)S(1)} %fusion.19, f32[3,512,256]{2,1,0:T(8,128)S(1)} %fusion.4, f32[3,512,256]{2,1,0:T(8,128)S(1)} %fusion.22, ...), kind=kOutput, calls=%fused_computation.25 | convolution fusion | flops 609484800 | bytes 17696768 | tf_op jit(solution)/shard_map/ts,csf->ctf/dot_general | solution.py:40
  88.4 33.0 %reduce-scatter.2.cloned.1.call-done = f32[3,256,128]{1,2,0:T(8,128)} async-done(((f32[3,256,512]{1,2,0:T(8,128)}), f32[3,256,128]{1,2,0:T(8,128)}) %reduce-scatter.2.cloned.1.call-update) | async-done | bytes 393232 | tf_op jit(solution)/shard_map/reduce_scatter | solution.py:101
  121.5 1.2 subtract_convert_fusion.8
  123.5 0.2 fusion.27
  123.8 4.7 %collective-permute-start.10 = (f32[3,64,128]{2,1,0:T(8,128)S(1)}, f32[3,64,128]{2,1,0:T(8,128)S(1)}, u32[]{:S(2)}, u32[]{:S(2)}) collective-permute-start(f32[3,64,128]{2,1,0:T(8,128)S(1)} %fusion.27), channel_id=1, source_target_pairs={{0,8},{4,12},{8,16},{12,20},{16,24},{20,28},{24,32},{28,36},{32,40... | collective-permute-start | bytes 294920 | tf_op jit(solution)/shard_map/ppermute | solution.py:12
  128.6 1.9 %collective-permute-start.11 = (f32[3,64,128]{2,1,0:T(8,128)S(1)}, f32[3,64,128]{2,1,0:T(8,128)S(1)}, u32[]{:S(2)}, u32[]{:S(2)}) collective-permute-start(f32[3,64,128]{2,1,0:T(8,128)S(1)} %fusion.26), channel_id=1, source_target_pairs={{0,4},{4,8},{8,12},{12,16},{16,20},{20,24},{24,28},{28,32},{32,36}... | collective-permute-start | bytes 294920 | tf_op jit(solution)/shard_map/ppermute | solution.py:12
  130.8 3.6 %collective-permute-start.12 = (f32[3,64,128]{2,1,0:T(8,128)S(1)}, f32[3,64,128]{2,1,0:T(8,128)S(1)}, u32[]{:S(2)}, u32[]{:S(2)}) collective-permute-start(f32[3,64,128]{2,1,0:T(8,128)S(1)} %fusion.25), channel_id=1, source_target_pairs={{4,0},{8,4},{12,8},{16,12},{20,16},{24,20},{28,24},{32,28},{36,32}... | collective-permute-start | bytes 294920 | tf_op jit(solution)/shard_map/ppermute | solution.py:12
  134.6 1.9 %collective-permute-start.13 = (f32[3,64,128]{2,1,0:T(8,128)S(1)}, f32[3,64,128]{2,1,0:T(8,128)S(1)}, u32[]{:S(2)}, u32[]{:S(2)}) collective-permute-start(f32[3,64,128]{2,1,0:T(8,128)S(1)} %fusion.24), channel_id=1, source_target_pairs={{8,0},{12,4},{16,8},{20,12},{24,16},{28,20},{32,24},{36,28},{40,32... | collective-permute-start | bytes 294920 | tf_op jit(solution)/shard_map/ppermute | solution.py:12
  136.6 0.9 copy.26
  137.5 7.0 %collective-permute-done.13 = f32[3,64,128]{2,1,0:T(8,128)S(1)} collective-permute-done((f32[3,64,128]{2,1,0:T(8,128)S(1)}, f32[3,64,128]{2,1,0:T(8,128)S(1)}, u32[]{:S(2)}, u32[]{:S(2)}) %collective-permute-start.13) | collective-permute-done | bytes 98336 | tf_op jit(solution)/shard_map/ppermute | solution.py:12
  144.5 0.8 pad_maximum_fusion.1
  (40 shorter events, 1.9 us)
Async XLA Ops:
  7.2 4.4 %copy-start.4 = (s32[256]{0:T(256)S(1)}, s32[256]{0:T(256)}, u32[]{:S(2)}) copy-start(s32[256]{0:T(256)} %param.8) | copy-start | bytes 3076
  7.2 14.5 %copy-start.3 = (s32[256,189]{0,1:T(8,128)S(1)}, s32[256,189]{0,1:T(8,128)}, u32[]{:S(2)}) copy-start(s32[256,189]{0,1:T(8,128)} %param.10) | copy-start | bytes 580612
  7.2 14.5 %copy-start.2 = (s32[256,189]{0,1:T(8,128)S(1)}, s32[256,189]{0,1:T(8,128)}, u32[]{:S(2)}) copy-start(s32[256,189]{0,1:T(8,128)} %param.9) | copy-start | bytes 580612
  7.2 114.3 %reduce-scatter.2.cloned.1.call-start = ((), (), s32[]{:S(2)}) async-start(), calls=%async_computation.1 | async-start | bytes 1966080 | tf_op jit(solution)/shard_map/reduce_scatter | solution.py:101
  9.6 28.1 %collective-permute-start.5 = (f32[3,64,512]{2,1,0:T(8,128)}, f32[3,64,512]{2,1,0:T(8,128)S(1)}, u32[]{:S(2)}, u32[]{:S(2)}) collective-permute-start(f32[3,64,512]{2,1,0:T(8,128)} %get-tuple-element.9), channel_id=1, source_target_pairs={{0,4},{4,8},{8,12},{12,16},{16,20},{20,24},{24,28},{28,32},{32,36}... | collective-permute-start | bytes 1179656 | tf_op jit(solution)/shard_map/ppermute | solution.py:12
  11.6 10.4 %collective-permute-start = (f32[64]{0:T(128)S(1)}, f32[64]{0:T(128)S(1)}, u32[]{:S(2)}, u32[]{:S(2)}) collective-permute-start(f32[64]{0:T(128)S(1)} %get-tuple-element.12), channel_id=1, source_target_pairs={{8,0},{12,4},{16,8},{20,12},{24,16},{28,20},{32,24},{36,28},{40,32... | collective-permute-start | bytes 776 | tf_op jit(solution)/shard_map/ppermute | solution.py:12
  14.3 25.4 %collective-permute-start.1 = (f32[3,64,512]{2,1,0:T(8,128)S(1)}, f32[3,64,512]{2,1,0:T(8,128)S(1)}, u32[]{:S(2)}, u32[]{:S(2)}) collective-permute-start(f32[3,64,512]{2,1,0:T(8,128)S(1)} %get-tuple-element.6), channel_id=1, source_target_pairs={{8,0},{12,4},{16,8},{20,12},{24,16},{28,20},{32,24},{36,28},{40,32... | collective-permute-start | bytes 1179656 | tf_op jit(solution)/shard_map/ppermute | solution.py:12
  16.7 8.5 %collective-permute-start.2 = (f32[64]{0:T(128)S(1)}, f32[64]{0:T(128)S(1)}, u32[]{:S(2)}, u32[]{:S(2)}) collective-permute-start(f32[64]{0:T(128)S(1)} %get-tuple-element.13), channel_id=1, source_target_pairs={{4,0},{8,4},{12,8},{16,12},{20,16},{24,20},{28,24},{32,28},{36,32}... | collective-permute-start | bytes 776 | tf_op jit(solution)/shard_map/ppermute | solution.py:12
  19.7 18.9 %collective-permute-start.3 = (f32[3,64,512]{2,1,0:T(8,128)S(1)}, f32[3,64,512]{2,1,0:T(8,128)S(1)}, u32[]{:S(2)}, u32[]{:S(2)}) collective-permute-start(f32[3,64,512]{2,1,0:T(8,128)S(1)} %get-tuple-element.7), channel_id=1, source_target_pairs={{4,0},{8,4},{12,8},{16,12},{20,16},{24,20},{28,24},{32,28},{36,32}... | collective-permute-start | bytes 1179656 | tf_op jit(solution)/shard_map/ppermute | solution.py:12
  22.1 9.9 %collective-permute-start.4 = (f32[64]{0:T(128)S(1)}, f32[64]{0:T(128)S(1)}, u32[]{:S(2)}, u32[]{:S(2)}) collective-permute-start(f32[64]{0:T(128)S(1)} %get-tuple-element.15), channel_id=1, source_target_pairs={{0,4},{4,8},{8,12},{12,16},{16,20},{20,24},{24,28},{28,32},{32,36}... | collective-permute-start | bytes 776 | tf_op jit(solution)/shard_map/ppermute | solution.py:12
  25.1 12.6 %collective-permute-start.6 = (f32[64]{0:T(128)S(1)}, f32[64]{0:T(128)S(1)}, u32[]{:S(2)}, u32[]{:S(2)}) collective-permute-start(f32[64]{0:T(128)S(1)} %get-tuple-element.14), channel_id=1, source_target_pairs={{0,8},{4,12},{8,16},{12,20},{16,24},{20,28},{24,32},{28,36},{32,40... | collective-permute-start | bytes 776 | tf_op jit(solution)/shard_map/ppermute | solution.py:12
  32.0 13.8 %collective-permute-start.7 = (f32[3,64,512]{2,1,0:T(8,128)S(1)}, f32[3,64,512]{2,1,0:T(8,128)S(1)}, u32[]{:S(2)}, u32[]{:S(2)}) collective-permute-start(f32[3,64,512]{2,1,0:T(8,128)S(1)} %get-tuple-element.8), channel_id=1, source_target_pairs={{0,8},{4,12},{8,16},{12,20},{16,24},{20,28},{24,32},{28,36},{32,40... | collective-permute-start | bytes 1179656 | tf_op jit(solution)/shard_map/ppermute | solution.py:12
  40.1 6.1 %copy-start.1 = (f32[3,256,512]{2,1,0:T(8,128)S(1)}, f32[3,256,512]{2,1,0:T(8,128)}, u32[]{:S(2)}) copy-start(f32[3,256,512]{2,1,0:T(8,128)} %param.6) | copy-start | bytes 4718596
  47.5 19.9 %collective-permute-start.8 = (bf16[3,256,512]{2,1,0:T(8,128)(2,1)S(1)}, bf16[3,256,512]{2,1,0:T(8,128)(2,1)}, u32[]{:S(2)}, u32[]{:S(2)}) collective-permute-start(bf16[3,256,512]{2,1,0:T(8,128)(2,1)S(1)} %fusion.9), channel_id=1, source_target_pairs={{0,4},{4,8},{8,12},{12,16},{16,20},{20,24},{24,28},{28,32},{32,36}... | collective-permute-start | bytes 2359304 | tf_op jit(solution)/shard_map/ppermute | solution.py:20
  49.5 17.8 %collective-permute-start.9 = (bf16[3,256,512]{2,1,0:T(8,128)(2,1)S(1)}, bf16[3,256,512]{2,1,0:T(8,128)(2,1)}, u32[]{:S(2)}, u32[]{:S(2)}) collective-permute-start(bf16[3,256,512]{2,1,0:T(8,128)(2,1)S(1)} %fusion.9), channel_id=1, source_target_pairs={{4,0},{8,4},{12,8},{16,12},{20,16},{24,20},{28,24},{32,28},{36,32}... | collective-permute-start | bytes 2359304 | tf_op jit(solution)/shard_map/ppermute | solution.py:23
  71.2 1.6 %copy-start.5 = (bf16[4,512,512]{2,1,0:T(8,128)(2,1)S(1)}, bf16[4,512,512]{2,1,0:T(8,128)(2,1)}, u32[]{:S(2)}) copy-start(bf16[4,512,512]{2,1,0:T(8,128)(2,1)} %param.11) | copy-start | bytes 6291460
  121.5 15.1 %copy-start = (f32[3,256,128]{1,2,0:T(8,128)S(1)}, f32[3,256,128]{1,2,0:T(8,128)}, u32[]{:S(2)}) copy-start(f32[3,256,128]{1,2,0:T(8,128)} %reduce-scatter.2.cloned.1.call-done) | copy-start | bytes 1179652
  123.8 13.7 %collective-permute-start.10 = (f32[3,64,128]{2,1,0:T(8,128)S(1)}, f32[3,64,128]{2,1,0:T(8,128)S(1)}, u32[]{:S(2)}, u32[]{:S(2)}) collective-permute-start(f32[3,64,128]{2,1,0:T(8,128)S(1)} %fusion.27), channel_id=1, source_target_pairs={{0,8},{4,12},{8,16},{12,20},{16,24},{20,28},{24,32},{28,36},{32,40... | collective-permute-start | bytes 294920 | tf_op jit(solution)/shard_map/ppermute | solution.py:12
  128.6 8.8 %collective-permute-start.11 = (f32[3,64,128]{2,1,0:T(8,128)S(1)}, f32[3,64,128]{2,1,0:T(8,128)S(1)}, u32[]{:S(2)}, u32[]{:S(2)}) collective-permute-start(f32[3,64,128]{2,1,0:T(8,128)S(1)} %fusion.26), channel_id=1, source_target_pairs={{0,4},{4,8},{8,12},{12,16},{16,20},{20,24},{24,28},{28,32},{32,36}... | collective-permute-start | bytes 294920 | tf_op jit(solution)/shard_map/ppermute | solution.py:12
  130.8 6.7 %collective-permute-start.12 = (f32[3,64,128]{2,1,0:T(8,128)S(1)}, f32[3,64,128]{2,1,0:T(8,128)S(1)}, u32[]{:S(2)}, u32[]{:S(2)}) collective-permute-start(f32[3,64,128]{2,1,0:T(8,128)S(1)} %fusion.25), channel_id=1, source_target_pairs={{4,0},{8,4},{12,8},{16,12},{20,16},{24,20},{28,24},{32,28},{36,32}... | collective-permute-start | bytes 294920 | tf_op jit(solution)/shard_map/ppermute | solution.py:12
  134.6 9.8 %collective-permute-start.13 = (f32[3,64,128]{2,1,0:T(8,128)S(1)}, f32[3,64,128]{2,1,0:T(8,128)S(1)}, u32[]{:S(2)}, u32[]{:S(2)}) collective-permute-start(f32[3,64,128]{2,1,0:T(8,128)S(1)} %fusion.24), channel_id=1, source_target_pairs={{8,0},{12,4},{16,8},{20,12},{24,16},{28,20},{32,24},{36,28},{40,32... | collective-permute-start | bytes 294920 | tf_op jit(solution)/shard_map/ppermute | solution.py:12
Sparse Core Ops, SparseCore 0:
  88.6 32.8 reduce-scatter.1
where the time goes:
time: 153 us; the launch traced here: 152 us
  waiting for transfers between devices  45.7 us (30%)
  starting transfers between devices  44.6 us (29%)
  matrix products  39.4 us (26%)
  between operations  14.5 us (9%)
  local copies, waits for them, and re-layouts  4.61 us (3%)
  other arithmetic  3.22 us (2%)
    ppermute x12, starting transfers between devices, passed_along(): lax.ppermute(value, axis, [(source, source + steps) for source in range(f...  39 us
    reduce_scatter x1, waiting for transfers between devices, on_device(): lax.psum_scatter(summed, 'pair', scatter_dimension=2, tiled=True)  33 us
    dot_general x1, matrix products, count_table(): jnp.einsum('tjh,tjl->thl', high_onehot, low_onehot, preferred_element_typ...  12.9 us
    ppermute x12, waiting for transfers between devices, passed_along(): lax.ppermute(value, axis, [(source, source + steps) for source in range(f...  12.7 us
    dot_general x4, matrix products, add_reflection(): jnp.einsum('cse,ef->csf', window, operator, preferred_element_type=jnp.fl...  11.3 us
    dot_general x12, matrix products, split_einsum(): jnp.einsum(form, exact_side, upper, preferred_element_type=jnp.float32)  8.2 us
    dot_general x12, matrix products, split_einsum(): jnp.einsum(form, exact_side, lower, preferred_element_type=jnp.float32)  6.96 us
    ppermute x1, starting transfers between devices, padded(): lax.ppermute(lax.slice_in_dim(block, 0, width, axis=dim), axis, backward)  3.54 us
  transfers between devices with their start and end apart: 15, of which 4 were waited for; matrix products, arithmetic and copies ran while one was open for 13% of the time, Pallas kernels for 0%

commit v1 on v0

v1 whole, which is shorter than its diff:
```python
import jax
import jax.numpy as jnp
from jax import lax
from jax.experimental import pallas as pl
from jax.experimental.pallas import tpu as pltpu
from jax.sharding import PartitionSpec as P

BOX = 256
CAPS = 64
E = 512
COLS = 128
REFL = 16
SLOTS = 3 * REFL
MSG = 3 * CAPS + 16
BF = jnp.bfloat16
F32 = jnp.float32
ANY = pl.BlockSpec(memory_space=pl.ANY)
SMEM = pl.BlockSpec(memory_space=pltpu.SMEM)
VMEM = pl.BlockSpec(memory_space=pltpu.VMEM)


def params(mib=48):
    return pltpu.CompilerParams(vmem_limit_bytes=mib << 20)


def cost(flops, nbytes):
    return pl.CostEstimate(flops=int(flops), bytes_accessed=int(nbytes), transcendentals=0)


def swapped(value, pairs, count):
    target = list(range(count))
    for a, b in pairs:
        target[a], target[b] = b, a
    return lax.ppermute(value, "cube", list(enumerate(target)))


def neighbours(count):
    same = [(i, i + 1) for i in range(0, count, 2)]
    across = [(i, i + 1) for i in range(1, count - 1, 2)]
    even = [(i + c, i + 2 + c) for i in range(0, count - 2, 4) for c in (0, 1)]
    odd = [(i + c, i + 2 + c) for i in range(2, count - 2, 4) for c in (0, 1)]
    return same, across, even, odd


def pack_kernel(meta, spill, labels, *outs):
    for m, out in enumerate(outs):
        group = meta[m]
        rows = pl.ds(pl.multiple_of(group * CAPS, CAPS), CAPS)
        for c in range(3):
            out[c * CAPS : (c + 1) * CAPS, :] = spill[c, rows, :].astype(BF)
        out[3 * CAPS :, :] = jnp.broadcast_to(labels[pl.ds(group, 1), :], (16, E)).astype(BF)


def pack(meta, spill, labels):
    return pl.pallas_call(
        pack_kernel,
        in_specs=[SMEM, VMEM, VMEM],
        out_specs=[VMEM] * 4,
        out_shape=[jax.ShapeDtypeStruct((MSG, E), BF)] * 4,
        compiler_params=params(),
        cost_estimate=cost(1e6, 2.4e6),
        name="pack",
    )(meta, spill, labels)


TB = 32
TG = 16


def table_kernel(hi_ref, lo_ref, *rest):
    out_ref = rest[-1]
    hi_ids = lax.broadcasted_iota(jnp.int32, (SLOTS, 256), 0).astype(BF)
    lo_ids = lax.broadcasted_iota(jnp.int32, (BOX, 256), 0).astype(BF)
    one, zero = jnp.ones((), BF), jnp.zeros((), BF)
    for g in range(TB // TG):
        found = []
        for u in range(TG):
            t = g * TG + u
            high = jnp.where(hi_ids == hi_ref[t : t + 1, :].astype(BF), one, zero)
            low = jnp.where(lo_ids == lo_ref[t : t + 1, :].astype(BF), one, zero)
            found.append(
                lax.dot_general(
                    high, low, (((1,), (1,)), ((), ())), preferred_element_type=F32
                )
            )
        stacked = jnp.transpose(jnp.stack(found, 0), (1, 0, 2))
        out_ref[:, g * TG : (g + 1) * TG, :] = stacked.astype(BF)


def table(hi, lo, first, steps, into=None):
    extra = [] if into is None else [into]
    return pl.pallas_call(
        table_kernel,
        grid=(steps,),
        in_specs=[pl.BlockSpec((TB, 256), lambda i: (i + first, 0))] * 2 + [ANY] * len(extra),
        out_specs=pl.BlockSpec((SLOTS, TB, BOX), lambda i: (0, i + first, 0)),
        out_shape=jax.ShapeDtypeStruct((SLOTS, BOX, BOX), BF),
        input_output_aliases={2: 0} if extra else {},
        compiler_params=params(),
        cost_estimate=cost(steps * 1.2e9, 1e6 * steps),
        name="table",
    )(hi, lo, *extra)


def gather_kernel(own, *refs):
    messages, out, pick = refs[:4], refs[4], refs[5]
    lane = lax.broadcasted_iota(jnp.int32, (1, 256), 1) // CAPS
    label = jnp.zeros((1, 256), F32)
    for m, msg in enumerate(messages):
        label = jnp.where(lane == m, msg[3 * CAPS :, :256].astype(F32)[:1], label)
    boxes = lax.broadcasted_iota(jnp.int32, (BOX, 256), 0).astype(F32)
    picker = jnp.where(boxes == label, 1.0, 0.0).astype(BF)
    pick[...] = picker
    for c in range(3):
        rows = jnp.concatenate([msg[c * CAPS : (c + 1) * CAPS, :] for msg in messages], axis=0)
        total = own[c] + jnp.dot(picker, rows, preferred_element_type=F32)
        out[c] = total.astype(BF)


def gather(own, messages):
    return pl.pallas_call(
        gather_kernel,
        in_specs=[VMEM] * 5,
        out_specs=[VMEM] * 2,
        out_shape=[
            jax.ShapeDtypeStruct((3, BOX, E), BF),
            jax.ShapeDtypeStruct((BOX, 4 * CAPS), BF),
        ],
        compiler_params=params(),
        cost_estimate=cost(2e8, 3.3e6),
        name="gather",
    )(own, *messages)


def apply_kernel(first, count, last, *refs):
    sign, refs = refs[0], refs[1:]
    windows, refs = refs[:count], refs[count:]
    ops, counts, refs = refs[:7], refs[7], refs[8:]
    if last:
        before, pick, own_out, picks, refs = refs[0], refs[1], refs[2], refs[3:7], refs[7:]
        total = refs[0]
        refs = refs[1:]
    else:
        total, refs = refs[0], refs[1:]
    win_v, op_v, count_v, win_sem, op_sem, count_sem = refs
    win_copies = [
        pltpu.make_async_copy(windows[b], win_v.at[b], win_sem.at[b]) for b in range(count)
    ]
    op_copies, at = [], 0
    for n, ref in enumerate(ops):
        size = ref.shape[0]
        op_copies.append(pltpu.make_async_copy(ref, op_v.at[pl.ds(at, size)], op_sem.at[n]))
        at += size
    count_copies = [
        pltpu.make_async_copy(
            counts.at[pl.ds((first + b) * REFL + half * 8, 8)],
            count_v.at[pl.ds(b * REFL + half * 8, 8)],
            count_sem.at[b * 2 + half],
        )
        for b in range(count)
        for half in range(2)
    ]
    win_copies[0].start()
    op_copies[0].start()
    count_copies[0].start()
    for copy in op_copies[1:] + count_copies[1:] + win_copies[1:]:
        copy.start()
    total[...] = before[...] if last else jnp.zeros_like(total)
    due = {0: 0, 2: 1, 3: 2, 4: 3, 5: 4, 6: 5, 7: 6}
    for b in range(count):
        win_copies[b].wait()
        window = jnp.concatenate([win_v[b, c] for c in range(3)], axis=0)
        for step in range(REFL // 2):
            if b == 0 and step in due:
                op_copies[due[step]].wait()
            if step % 4 == 0:
                count_copies[b * 2 + step // 4].wait()
            r = 2 * step
            operator = jnp.concatenate([op_v[r], op_v[r + 1]], axis=1)
            moved = jnp.dot(window, operator, preferred_element_type=F32)
            rows = []
            for u in range(2):
                rows.append(
                    jnp.concatenate(
                        [
                            (
                                sign[(r + u) * 3 + c]
                                * moved[c * BOX : (c + 1) * BOX, u * COLS : (u + 1) * COLS]
                            ).astype(BF)
                            for c in range(3)
                        ],
                        axis=1,
                    )
                )
            lhs = jnp.concatenate(
                [count_v[b * REFL + r], count_v[b * REFL + r + 1]], axis=1
            )
            total[...] += jnp.dot(
                lhs, jnp.concatenate(rows, axis=0), preferred_element_type=F32
            )
    if last:
        summed = total[...]
        for c in range(3):
            own_out[c] = summed[:, c * COLS : (c + 1) * COLS]
        picked = lax.dot_general(
            pick[...], summed.astype(BF), (((0,), (0,)), ((), ())), preferred_element_type=F32
        ).astype(BF)
        for m in range(4):
            picks[m][...] = picked[m * CAPS : (m + 1) * CAPS]


def apply(sign, windows, ops, counts, first, last=()):
    count = len(windows)
    total = jax.ShapeDtypeStruct((BOX, 3 * COLS), F32)
    picks = [jax.ShapeDtypeStruct((CAPS, 3 * COLS), BF)] * 4
    own = jax.ShapeDtypeStruct((3, BOX, COLS), F32)
    scratch = [
        pltpu.VMEM((count, 3, BOX, E), BF),
        pltpu.VMEM((REFL, E, COLS), BF),
        pltpu.VMEM((count * REFL, BOX, BOX), BF),
        pltpu.SemaphoreType.DMA((count,)),
        pltpu.SemaphoreType.DMA((7,)),
        pltpu.SemaphoreType.DMA((count * 2,)),
    ]
    if last:
        scratch = [pltpu.VMEM((BOX, 3 * COLS), F32)] + scratch

    def kernel(*refs):
        apply_kernel(first, count, bool(last), *refs)

    return pl.pallas_call(
        kernel,
        in_specs=[SMEM] + [ANY] * (count + 8) + [VMEM] * len(last),
        out_specs=[VMEM] * 5 if last else VMEM,
        out_shape=[own] + picks if last else total,
        scratch_shapes=scratch,
        compiler_params=params(),
        cost_estimate=cost(count * 2.4e9, count * 3e6 + 2e6),
        name="apply_last" if last else "apply_first",
    )(sign, *windows, *ops, counts, *last)


def place_kernel(meta, *refs):
    out = refs[4]
    for m in range(4):
        rows = pl.ds(pl.multiple_of(meta[m] * CAPS, CAPS), CAPS)
        for c in range(3):
            out[c, rows, :] = refs[m][:, c * COLS : (c + 1) * COLS].astype(F32)


def place(meta, messages):
    return pl.pallas_call(
        place_kernel,
        in_specs=[SMEM] + [VMEM] * 4,
        out_specs=VMEM,
        out_shape=jax.ShapeDtypeStruct((3, 4 * CAPS, COLS), F32),
        compiler_params=params(),
        cost_estimate=cost(1e5, 6e5),
        name="place",
    )(meta, *messages)


def on_device(own_partial, spill_partial, spill_box, sources, reflections, operators):
    cube, pair = lax.axis_index("cube"), lax.axis_index("pair")
    count, pairs = lax.axis_size("cube"), lax.axis_size("pair")
    core, chip_odd = cube & 1, (cube >> 1) & 1
    chip = cube >> 1
    routes = neighbours(count)

    meta = jnp.stack([2 - core, 1 + core, 3 - 3 * chip_odd, 3 * chip_odd])
    offsets = jnp.array([-2, -1, 1, 2], jnp.int32)[:, None]
    there = (cube + offsets >= 0) & (cube + offsets < count)
    labels = jnp.where(there, spill_box.reshape(4, CAPS), -1).astype(F32)
    messages = pack(meta, spill_partial, jnp.tile(labels, (1, E // CAPS)))
    order = (1, 2, 3, 0)
    got = [None] * 4
    for m in order:
        got[m] = swapped(messages[m], routes[m], count)

    held = operators.shape[0]
    mine = lax.dynamic_slice(operators, (0, 0, COLS * pair), (held, E, COLS))
    direct = []
    for k in range(1, pairs):
        target = (pair - k) % pairs
        part = lax.dynamic_slice(operators, (2 * core, 0, COLS * target), (2, E, COLS))
        direct.append(
            lax.ppermute(part, "pair", [(s, (s - k) % pairs) for s in range(pairs)])
        )
    other = [swapped(part, routes[0], count) for part in direct]
    ops = [mine] + direct + other

    block = (sources >> 8) - cube
    block = jnp.where(block == 0, 0, jnp.where(block == 1 - 2 * core, 1, 2))
    k = ((reflections >> 2) - pair) & 3
    within = reflections & 3
    far = 2 * k + (within & 1) + jnp.where((within >> 1) == core, 2, 8)
    slot = jnp.where(k == 0, within, far)
    width = 256 - sources.shape[1]
    hi = jnp.pad((block * REFL + slot).astype(F32), ((0, 0), (0, width)), constant_values=-1)
    lo = jnp.pad((sources & 255).astype(F32), ((0, 0), (0, width)))
    slots = jnp.arange(REFL, dtype=jnp.int32)
    step = jnp.where(slots < 10, slots - 4, slots - 10)
    half = jnp.where(slots < 10, core, 1 - core)
    refl = 4 * ((pair + 1 + (step >> 1)) & 3) + 2 * half + (step & 1)
    refl = jnp.where(slots < 4, 4 * pair + slots, refl)
    bits = jnp.arange(3, dtype=jnp.int32)
    sign = (1 - 2 * ((refl[:, None] >> bits) & 1)).astype(F32).reshape(-1)

    steps = BOX // TB
    counts = table(hi, lo, 0, steps // 2)
    multipole, picker = gather(own_partial, got)
    across = swapped(multipole, routes[1], count)
    same = swapped(multipole, routes[0], count)
    hi, lo, _ = lax.optimization_barrier((hi, lo, multipole))
    counts = table(hi, lo, steps // 2, steps - steps // 2, counts)
    total = apply(sign, [multipole, same], ops, counts, 0)
    local_own, *picks = apply(sign, [across], ops, counts, 2, (total, picker))
    back = [None] * 4
    for m in order:
        back[m] = swapped(picks[m], routes[m], count)
    return local_own, place(meta, back)


def solution(mesh):
    in_specs = (
        P(None, "cube", None),
        P(None, "cube", None),
        P("cube"),
        P("cube", None),
        P("cube", None),
        P("pair", None, None),
    )
    out_specs = (P(None, "cube", "pair"), P(None, "cube", "pair"))
    return jax.shard_map(
        on_device, mesh=mesh, in_specs=in_specs, out_specs=out_specs, check_vma=False
    )
```

time: 153 us -> 85.9 us (0.56)
  the two profiles are of different devices: /device:TPU:120 before, /device:TPU:134 now
where the time goes in v1:
time: 85.9 us; the launch traced here: 85.4 us
  Pallas kernels  41.6 us (48%)
  starting transfers between devices  25.2 us (29%)
  waiting for transfers between devices  10.1 us (12%)
  local copies, waits for them, and re-layouts  6.4 us (7%)
  other arithmetic  1.11 us (1%)
  between operations  0.93 us (1%)
    pallas_call x2, Pallas kernels, apply(): pl.pallas_call(kernel, in_specs=[SMEM] + [ANY] * (count + 8) + [VMEM] * l...  23.6 us
    ppermute x13, starting transfers between devices, swapped(): return lax.ppermute(value, 'cube', list(enumerate(target)))  21.7 us
    pallas_call x2, Pallas kernels, table(): pl.pallas_call(table_kernel, grid=(steps,), in_specs=[pl.BlockSpec((TB, 2...  13.1 us
    ppermute x13, waiting for transfers between devices, swapped(): return lax.ppermute(value, 'cube', list(enumerate(target)))  7.39 us
    ppermute x3, starting transfers between devices, on_device(): lax.ppermute(part, 'pair', [(s, (s - k) % pairs) for s in range(pairs)])  3.51 us
    ppermute x3, waiting for transfers between devices, on_device(): lax.ppermute(part, 'pair', [(s, (s - k) % pairs) for s in range(pairs)])  2.74 us
    unnamed x14, local copies, waits for them, and re-layouts  2.33 us
    pallas_call x1, Pallas kernels, gather(): pl.pallas_call(gather_kernel, in_specs=[VMEM] * 5, out_specs=[VMEM] * 2,...  2.2 us
  transfers between devices with their start and end apart: 16, of which 4 were waited for; matrix products, arithmetic and copies ran while one was open for 4% of the time, Pallas kernels for 35%

profile of v1, /device:TPU:134, one launch (start us, length us, event | category | flops | bytes accessed | tf_op | source)
XLA Modules:
  0.0 85.4 jit_solution(1957013998257705158)
XLA Ops:
  0.6 0.7 compare_and_fusion
  1.3 0.8 reshape.64
  2.1 0.1 select_convert_fusion
  2.1 0.1 tile.10.labels
  2.2 0.1 pad_add_fusion.meta
  2.3 1.4 %copy-done = f32[3,256,512]{2,1,0:T(8,128)S(1)} copy-done((f32[3,256,512]{2,1,0:T(8,128)S(1)}, f32[3,256,512]{2,1,0:T(8,128)}, u32[]{:S(2)}) %copy-start) | copy-done | bytes 1572888
  3.7 1.4 %pack.1 = (bf16[208,512]{1,0:T(8,128)(2,1)S(1)}, bf16[208,512]{1,0:T(8,128)(2,1)S(1)}, bf16[208,512]{1,0:T(8,128)(2,1)}, bf16[208,512]{1,0:T(8,128)(2,1)}) custom-call(s32[4]{0:T(128)S(1)} %pad_add_fusion.meta, f32[3,256,512]{2,1,0:T(8,128)S(1)} %copy-done, f32[4,512]{1,0:T(4,128)S(1)} %tile.10.labels), custom_call_target="tpu_custom_call" | custom-call | flops 1000000 | bytes 2400000 | tf_op jit(solution)/shard_map/pack/pallas_call | solution.py:55
  5.1 0.0 collective-permute-start
  5.1 4.6 %collective-permute-start.1 = (bf16[208,512]{1,0:T(8,128)(2,1)S(1)}, bf16[208,512]{1,0:T(8,128)(2,1)S(1)}, u32[]{:S(2)}, u32[]{:S(2)}) collective-permute-start(bf16[208,512]{1,0:T(8,128)(2,1)S(1)} %get-tuple-element.16), channel_id=1, source_target_pairs={{0,0},{4,8},{8,4},{12,16},{16,12},{20,24},{24,20},{28,32},{32,28},... | collective-permute-start | bytes 638984 | tf_op jit(solution)/shard_map/ppermute | solution.py:34
  9.7 0.1 collective-permute-start.2
  9.8 3.1 %collective-permute-start.3 = (bf16[208,512]{1,0:T(8,128)(2,1)}, bf16[208,512]{1,0:T(8,128)(2,1)}, u32[]{:S(2)}, u32[]{:S(2)}) collective-permute-start(bf16[208,512]{1,0:T(8,128)(2,1)} %get-tuple-element.18), channel_id=1, source_target_pairs={{0,0},{4,4},{8,16},{12,20},{16,8},{20,12},{24,32},{28,36},{32,24},... | collective-permute-start | bytes 638984 | tf_op jit(solution)/shard_map/ppermute | solution.py:34
  12.9 2.0 %constant_dynamic-slice_fusion = (bf16[2,512,128]{2,1,0:T(8,128)(2,1)}, bf16[2,512,128]{2,1,0:T(8,128)(2,1)}, bf16[2,512,128]{2,1,0:T(8,128)(2,1)}) fusion(bf16[4,512,512]{2,1,0:T(8,128)(2,1)} %param.12, s32[]{:T(128)S(6)} %select_n.85, s32[]{:T(128)S(6)} %select_n.91, s32[]{:T(128)S(6)} %select_n.87, s32[]{:T(128)S(6)} %select_n.89), kind=kLoop, calls=%fused_computation.14 | loop fusion | bytes 1572880 | tf_op jit(solution)/shard_map/dynamic_slice | solution.py:285
  15.0 0.5 collective-permute-start.7
  15.4 0.1 copy.18
  15.6 0.1 copy.19
  15.7 0.2 and_convert_fusion
  16.0 0.0 copy-start.1
  16.0 6.6 %table.2.rest_0_ = bf16[48,256,256]{2,1,0:T(8,128)(2,1)} custom-call(f32[256,256]{1,0:T(8,128)S(1)} %pad.7.hi_ref, f32[256,256]{1,0:T(8,128)S(1)} %pad.8.lo_ref), custom_call_target="tpu_custom_call" | custom-call | flops 4800000000 | bytes 4000000 | tf_op jit(solution)/shard_map/table/pallas_call | solution.py:92
  22.6 1.6 %collective-permute-start.5 = (bf16[2,512,128]{2,1,0:T(8,128)(2,1)}, bf16[2,512,128]{2,1,0:T(8,128)(2,1)S(1)}, u32[]{:S(2)}, u32[]{:S(2)}) collective-permute-start(bf16[2,512,128]{2,1,0:T(8,128)(2,1)} %get-tuple-element.29), channel_id=1, source_target_pairs={{0,3},{1,0},{2,1},{3,2},{4,7},{5,4},{6,5},{7,6},{8,11},{9,8},{10,9... | collective-permute-start | bytes 786440 | tf_op jit(solution)/shard_map/ppermute | solution.py:287
  24.2 0.0 collective-permute-done.1.refs_1_
  24.2 1.4 %collective-permute-start.6 = (bf16[2,512,128]{2,1,0:T(8,128)(2,1)}, bf16[2,512,128]{2,1,0:T(8,128)(2,1)S(1)}, u32[]{:S(2)}, u32[]{:S(2)}) collective-permute-start(bf16[2,512,128]{2,1,0:T(8,128)(2,1)} %get-tuple-element.30), channel_id=1, source_target_pairs={{0,2},{1,3},{2,0},{3,1},{4,6},{5,7},{6,4},{7,5},{8,10},{9,11},{10,... | collective-permute-start | bytes 786440 | tf_op jit(solution)/shard_map/ppermute | solution.py:287
  25.7 2.2 %gather.1 = (bf16[3,256,512]{2,1,0:T(8,128)(2,1)}, bf16[256,256]{1,0:T(8,128)(2,1)S(1)}) custom-call(f32[3,256,512]{2,1,0:T(8,128)S(1)} %copy-done.1, bf16[208,512]{1,0:T(8,128)(2,1)S(1)} %collective-permute-done.refs_0_, bf16[208,512]{1,0:T(8,128)(2,1)S(1)} %collective-permute-done.1.refs_1_, bf16[208,512]{1,0:T(8,128)(2,1)S(1)} %collective-permute-done.2.refs_2_, ...), custom_call_target="tpu_custom_call" | custom-call | flops 200000000 | bytes 3300000 | tf_op jit(solution)/shard_map/gather/pallas_call | solution.py:121
  27.9 0.6 copy-done.2
  28.5 0.5 collective-permute-start.11
  29.0 0.1 subtract_convert_fusion
  29.1 0.1 reshape.65.refs_0_
  29.2 1.1 %constant_dynamic-slice_fusion.3.refs_3_.refs_2_ = bf16[4,512,128]{2,1,0:T(8,128)(2,1)S(1)} fusion(bf16[4,512,512]{2,1,0:T(8,128)(2,1)} %param.12, s32[]{:T(128)S(6)} %select_n.84), kind=kLoop, calls=%fused_computation.17 | loop fusion | bytes 1048580 | tf_op jit(solution)/shard_map/dynamic_slice | solution.py:281
  30.3 5.7 %collective-permute-start.4 = (bf16[3,256,512]{2,1,0:T(8,128)(2,1)}, bf16[3,256,512]{2,1,0:T(8,128)(2,1)S(1)}, u32[]{:S(2)}, u32[]{:S(2)}) collective-permute-start(bf16[3,256,512]{2,1,0:T(8,128)(2,1)} %get-tuple-element.19.refs_1_), channel_id=1, source_target_pairs={{0,0},{4,8},{8,4},{12,16},{16,12},{20,24},{24,20},{28,32},{32,28},... | collective-permute-start | bytes 2359304 | tf_op jit(solution)/shard_map/ppermute | solution.py:34
  36.0 0.0 collective-permute-done.7.refs_6_.refs_5_
  36.0 0.1 collective-permute-start.10
  36.1 2.7 %collective-permute-done.5.refs_4_.refs_3_ = bf16[2,512,128]{2,1,0:T(8,128)(2,1)S(1)} collective-permute-done((bf16[2,512,128]{2,1,0:T(8,128)(2,1)}, bf16[2,512,128]{2,1,0:T(8,128)(2,1)S(1)}, u32[]{:S(2)}, u32[]{:S(2)}) %collective-permute-start.5) | collective-permute-done | bytes 262176 | tf_op jit(solution)/shard_map/ppermute | solution.py:287
  38.8 0.2 collective-permute-start.8
  39.0 0.0 collective-permute-done.6.refs_5_.refs_4_
  39.0 0.3 collective-permute-start.9
  39.3 6.6 %table.3.refs_10_.refs_9_ = bf16[48,256,256]{2,1,0:T(8,128)(2,1)} custom-call(f32[256,256]{1,0:T(8,128)S(1)} %pad.7.hi_ref, f32[256,256]{1,0:T(8,128)S(1)} %pad.8.lo_ref, bf16[48,256,256]{2,1,0:T(8,128)(2,1)} %table.2.rest_0_), custom_call_target="tpu_custom_call", output_to_operand_aliasing={{}: (2, {})} | custom-call | flops 4800000000 | bytes 4000000 | tf_op jit(solution)/shard_map/table/pallas_call | solution.py:92
  45.9 0.0 collective-permute-done.8.refs_7_.refs_6_
  45.9 0.0 collective-permute-done.9.refs_8_.refs_7_
  45.9 0.0 collective-permute-done.11.refs_2_
  45.9 14.4 %apply_first.1.refs_10_ = f32[256,384]{1,0:T(8,128)S(1)} custom-call(f32[48]{0:T(128)S(1)} %reshape.65.refs_0_, bf16[3,256,512]{2,1,0:T(8,128)(2,1)} %get-tuple-element.19.refs_1_, bf16[3,256,512]{2,1,0:T(8,128)(2,1)S(1)} %collective-permute-done.11.refs_2_, bf16[4,512,128]{2,1,0:T(8,128)(2,1)S(1)} %constant_dynamic-slice_fusion.3.refs_3_.refs_2_, ...), custom_call_target="tpu_custom_call" | custom-call | flops 4800000000 | bytes 8000000 | tf_op jit(solution)/shard_map/apply_first/pallas_call | solution.py:231
  60.3 9.2 %apply_last.1 = (f32[3,256,128]{2,1,0:T(8,128)}, bf16[64,384]{1,0:T(8,128)(2,1)S(1)}, bf16[64,384]{1,0:T(8,128)(2,1)S(1)}, bf16[64,384]{1,0:T(8,128)(2,1)S(1)}, bf16[64,384]{1,0:T(8,128)(2,1)S(1)}) custom-call(f32[48]{0:T(128)S(1)} %reshape.65.refs_0_, bf16[3,256,512]{2,1,0:T(8,128)(2,1)S(1)} %collective-permute-done.4.refs_1_, ...), custom_call_target="tpu_custom_call" | custom-call | flops 2400000000 | bytes 5000000 | tf_op jit(solution)/shard_map/apply_last/pallas_call | solution.py:231
  69.5 0.3 collective-permute-start.12
  69.8 4.8 %collective-permute-start.13 = (bf16[64,384]{1,0:T(8,128)(2,1)S(1)}, bf16[64,384]{1,0:T(8,128)(2,1)S(1)}, u32[]{:S(2)}, u32[]{:S(2)}) collective-permute-start(bf16[64,384]{1,0:T(8,128)(2,1)S(1)} %get-tuple-element.25), channel_id=1, source_target_pairs={{0,0},{4,8},{8,4},{12,16},{16,12},{20,24},{24,20},{28,32},{32,28},... | collective-permute-start | bytes 147464 | tf_op jit(solution)/shard_map/ppermute | solution.py:34
  74.7 0.1 collective-permute-start.14
  74.8 1.9 %collective-permute-start.15 = (bf16[64,384]{1,0:T(8,128)(2,1)S(1)}, bf16[64,384]{1,0:T(8,128)(2,1)S(1)}, u32[]{:S(2)}, u32[]{:S(2)}) collective-permute-start(bf16[64,384]{1,0:T(8,128)(2,1)S(1)} %get-tuple-element.27), channel_id=1, source_target_pairs={{0,0},{4,4},{8,16},{12,20},{16,8},{20,12},{24,32},{28,36},{32,24},... | collective-permute-start | bytes 147464 | tf_op jit(solution)/shard_map/ppermute | solution.py:34
  76.7 1.8 %collective-permute-done.13.refs_1_ = bf16[64,384]{1,0:T(8,128)(2,1)S(1)} collective-permute-done((bf16[64,384]{1,0:T(8,128)(2,1)S(1)}, bf16[64,384]{1,0:T(8,128)(2,1)S(1)}, u32[]{:S(2)}, u32[]{:S(2)}) %collective-permute-start.13) | collective-permute-done | bytes 49184 | tf_op jit(solution)/shard_map/ppermute | solution.py:34
  78.6 0.3 collective-permute-done.14.refs_2_
  78.9 5.2 %collective-permute-done.15.refs_3_ = bf16[64,384]{1,0:T(8,128)(2,1)S(1)} collective-permute-done((bf16[64,384]{1,0:T(8,128)(2,1)S(1)}, bf16[64,384]{1,0:T(8,128)(2,1)S(1)}, u32[]{:S(2)}, u32[]{:S(2)}) %collective-permute-start.15) | collective-permute-done | bytes 49184 | tf_op jit(solution)/shard_map/ppermute | solution.py:34
  84.1 1.3 %place.1 = f32[3,256,128]{2,1,0:T(8,128)} custom-call(s32[4]{0:T(128)S(1)} %pad_add_fusion.meta, bf16[64,384]{1,0:T(8,128)(2,1)S(1)} %collective-permute-done.12.refs_0_, bf16[64,384]{1,0:T(8,128)(2,1)S(1)} %collective-permute-done.13.refs_1_, bf16[64,384]{1,0:T(8,128)(2,1)S(1)} %collective-permute-done.14.refs_2_, ...), custom_call_target="tpu_custom_call" | custom-call | flops 100000 | bytes 600000 | tf_op jit(solution)/shard_map/place/pallas_call | solution.py:252
  (19 shorter events, 0.1 us)
Async XLA Ops:
  2.3 1.4 %copy-start = (f32[3,256,512]{2,1,0:T(8,128)S(1)}, f32[3,256,512]{2,1,0:T(8,128)}, u32[]{:S(2)}) copy-start(f32[3,256,512]{2,1,0:T(8,128)} %spill.1) | copy-start | bytes 4718596
  3.7 11.7 %copy-start.4 = (s32[256,189]{0,1:T(8,128)S(1)}, s32[256,189]{0,1:T(8,128)}, u32[]{:S(2)}) copy-start(s32[256,189]{0,1:T(8,128)} %param.10) | copy-start | bytes 580612
  3.7 11.9 %copy-start.5 = (s32[256,189]{0,1:T(8,128)S(1)}, s32[256,189]{0,1:T(8,128)}, u32[]{:S(2)}) copy-start(s32[256,189]{0,1:T(8,128)} %param.11) | copy-start | bytes 580612
  5.1 17.5 %collective-permute-start = (bf16[208,512]{1,0:T(8,128)(2,1)S(1)}, bf16[208,512]{1,0:T(8,128)(2,1)S(1)}, u32[]{:S(2)}, u32[]{:S(2)}) collective-permute-start(bf16[208,512]{1,0:T(8,128)(2,1)S(1)} %get-tuple-element.15), channel_id=1, source_target_pairs={{0,4},{4,0},{8,12},{12,8},{16,20},{20,16},{24,28},{28,24},{32,36},... | collective-permute-start | bytes 638984 | tf_op jit(solution)/shard_map/ppermute | solution.py:34
  5.1 19.1 %collective-permute-start.1 = (bf16[208,512]{1,0:T(8,128)(2,1)S(1)}, bf16[208,512]{1,0:T(8,128)(2,1)S(1)}, u32[]{:S(2)}, u32[]{:S(2)}) collective-permute-start(bf16[208,512]{1,0:T(8,128)(2,1)S(1)} %get-tuple-element.16), channel_id=1, source_target_pairs={{0,0},{4,8},{8,4},{12,16},{16,12},{20,24},{24,20},{28,32},{32,28},... | collective-permute-start | bytes 638984 | tf_op jit(solution)/shard_map/ppermute | solution.py:34
  9.7 16.0 %collective-permute-start.2 = (bf16[208,512]{1,0:T(8,128)(2,1)}, bf16[208,512]{1,0:T(8,128)(2,1)S(1)}, u32[]{:S(2)}, u32[]{:S(2)}) collective-permute-start(bf16[208,512]{1,0:T(8,128)(2,1)} %get-tuple-element.17), channel_id=1, source_target_pairs={{0,8},{4,12},{8,0},{12,4},{16,24},{20,28},{24,16},{28,20},{32,40},... | collective-permute-start | bytes 638984 | tf_op jit(solution)/shard_map/ppermute | solution.py:34
  9.8 15.9 %collective-permute-start.3 = (bf16[208,512]{1,0:T(8,128)(2,1)}, bf16[208,512]{1,0:T(8,128)(2,1)}, u32[]{:S(2)}, u32[]{:S(2)}) collective-permute-start(bf16[208,512]{1,0:T(8,128)(2,1)} %get-tuple-element.18), channel_id=1, source_target_pairs={{0,0},{4,4},{8,16},{12,20},{16,8},{20,12},{24,32},{28,36},{32,24},... | collective-permute-start | bytes 638984 | tf_op jit(solution)/shard_map/ppermute | solution.py:34
  15.0 21.0 %collective-permute-start.7 = (bf16[2,512,128]{2,1,0:T(8,128)(2,1)}, bf16[2,512,128]{2,1,0:T(8,128)(2,1)S(1)}, u32[]{:S(2)}, u32[]{:S(2)}) collective-permute-start(bf16[2,512,128]{2,1,0:T(8,128)(2,1)} %get-tuple-element.28), channel_id=1, source_target_pairs={{0,1},{1,2},{2,3},{3,0},{4,5},{5,6},{6,7},{7,4},{8,9},{9,10},{10,1... | collective-permute-start | bytes 786440 | tf_op jit(solution)/shard_map/ppermute | solution.py:287
  16.0 9.7 %copy-start.1 = (f32[3,256,512]{2,1,0:T(8,128)S(1)}, f32[3,256,512]{2,1,0:T(8,128)}, u32[]{:S(2)}) copy-start(f32[3,256,512]{2,1,0:T(8,128)} %own.1) | copy-start | bytes 4718596
  22.6 16.2 %collective-permute-start.5 = (bf16[2,512,128]{2,1,0:T(8,128)(2,1)}, bf16[2,512,128]{2,1,0:T(8,128)(2,1)S(1)}, u32[]{:S(2)}, u32[]{:S(2)}) collective-permute-start(bf16[2,512,128]{2,1,0:T(8,128)(2,1)} %get-tuple-element.29), channel_id=1, source_target_pairs={{0,3},{1,0},{2,1},{3,2},{4,7},{5,4},{6,5},{7,6},{8,11},{9,8},{10,9... | collective-permute-start | bytes 786440 | tf_op jit(solution)/shard_map/ppermute | solution.py:287
  24.2 14.8 %collective-permute-start.6 = (bf16[2,512,128]{2,1,0:T(8,128)(2,1)}, bf16[2,512,128]{2,1,0:T(8,128)(2,1)S(1)}, u32[]{:S(2)}, u32[]{:S(2)}) collective-permute-start(bf16[2,512,128]{2,1,0:T(8,128)(2,1)} %get-tuple-element.30), channel_id=1, source_target_pairs={{0,2},{1,3},{2,0},{3,1},{4,6},{5,7},{6,4},{7,5},{8,10},{9,11},{10,... | collective-permute-start | bytes 786440 | tf_op jit(solution)/shard_map/ppermute | solution.py:287
  27.9 0.6 copy-start.2
  28.5 17.4 %collective-permute-start.11 = (bf16[3,256,512]{2,1,0:T(8,128)(2,1)}, bf16[3,256,512]{2,1,0:T(8,128)(2,1)S(1)}, u32[]{:S(2)}, u32[]{:S(2)}) collective-permute-start(bf16[3,256,512]{2,1,0:T(8,128)(2,1)} %get-tuple-element.19.refs_1_), channel_id=1, source_target_pairs={{0,4},{4,0},{8,12},{12,8},{16,20},{20,16},{24,28},{28,24},{32,36},... | collective-permute-start | bytes 2359304 | tf_op jit(solution)/shard_map/ppermute | solution.py:34
  30.3 30.0 %collective-permute-start.4 = (bf16[3,256,512]{2,1,0:T(8,128)(2,1)}, bf16[3,256,512]{2,1,0:T(8,128)(2,1)S(1)}, u32[]{:S(2)}, u32[]{:S(2)}) collective-permute-start(bf16[3,256,512]{2,1,0:T(8,128)(2,1)} %get-tuple-element.19.refs_1_), channel_id=1, source_target_pairs={{0,0},{4,8},{8,4},{12,16},{16,12},{20,24},{24,20},{28,32},{32,28},... | collective-permute-start | bytes 2359304 | tf_op jit(solution)/shard_map/ppermute | solution.py:34
  36.0 9.9 %collective-permute-start.10 = (bf16[2,512,128]{2,1,0:T(8,128)(2,1)S(1)}, bf16[2,512,128]{2,1,0:T(8,128)(2,1)S(1)}, u32[]{:S(2)}, u32[]{:S(2)}) collective-permute-start(bf16[2,512,128]{2,1,0:T(8,128)(2,1)S(1)} %collective-permute-done.7.refs_6_.refs_5_), channel_id=1, source_target_pairs={{0,4},{4,0},{8,12},{12,8},{16,20},{20,16},{24,28},{28,24},{32,36},... | collective-permute-start | bytes 786440 | tf_op jit(solution)/shard_map/ppermute | solution.py:34
  38.8 7.1 %collective-permute-start.8 = (bf16[2,512,128]{2,1,0:T(8,128)(2,1)S(1)}, bf16[2,512,128]{2,1,0:T(8,128)(2,1)S(1)}, u32[]{:S(2)}, u32[]{:S(2)}) collective-permute-start(bf16[2,512,128]{2,1,0:T(8,128)(2,1)S(1)} %collective-permute-done.5.refs_4_.refs_3_), channel_id=1, source_target_pairs={{0,4},{4,0},{8,12},{12,8},{16,20},{20,16},{24,28},{28,24},{32,36},... | collective-permute-start | bytes 786440 | tf_op jit(solution)/shard_map/ppermute | solution.py:34
  39.0 6.9 %collective-permute-start.9 = (bf16[2,512,128]{2,1,0:T(8,128)(2,1)S(1)}, bf16[2,512,128]{2,1,0:T(8,128)(2,1)S(1)}, u32[]{:S(2)}, u32[]{:S(2)}) collective-permute-start(bf16[2,512,128]{2,1,0:T(8,128)(2,1)S(1)} %collective-permute-done.6.refs_5_.refs_4_), channel_id=1, source_target_pairs={{0,4},{4,0},{8,12},{12,8},{16,20},{20,16},{24,28},{28,24},{32,36},... | collective-permute-start | bytes 786440 | tf_op jit(solution)/shard_map/ppermute | solution.py:34
  45.9 14.4 %copy-start.3 = (bf16[256,256]{1,0:T(8,128)(2,1)S(1)}, bf16[256,256]{1,0:T(8,128)(2,1)}, u32[]{:S(2)}) copy-start(bf16[256,256]{1,0:T(8,128)(2,1)} %copy-done.2) | copy-start | bytes 393220
  69.5 7.2 %collective-permute-start.12 = (bf16[64,384]{1,0:T(8,128)(2,1)S(1)}, bf16[64,384]{1,0:T(8,128)(2,1)S(1)}, u32[]{:S(2)}, u32[]{:S(2)}) collective-permute-start(bf16[64,384]{1,0:T(8,128)(2,1)S(1)} %get-tuple-element.24), channel_id=1, source_target_pairs={{0,4},{4,0},{8,12},{12,8},{16,20},{20,16},{24,28},{28,24},{32,36},... | collective-permute-start | bytes 147464 | tf_op jit(solution)/shard_map/ppermute | solution.py:34
  69.8 8.7 %collective-permute-start.13 = (bf16[64,384]{1,0:T(8,128)(2,1)S(1)}, bf16[64,384]{1,0:T(8,128)(2,1)S(1)}, u32[]{:S(2)}, u32[]{:S(2)}) collective-permute-start(bf16[64,384]{1,0:T(8,128)(2,1)S(1)} %get-tuple-element.25), channel_id=1, source_target_pairs={{0,0},{4,8},{8,4},{12,16},{16,12},{20,24},{24,20},{28,32},{32,28},... | collective-permute-start | bytes 147464 | tf_op jit(solution)/shard_map/ppermute | solution.py:34
  74.7 4.2 %collective-permute-start.14 = (bf16[64,384]{1,0:T(8,128)(2,1)S(1)}, bf16[64,384]{1,0:T(8,128)(2,1)S(1)}, u32[]{:S(2)}, u32[]{:S(2)}) collective-permute-start(bf16[64,384]{1,0:T(8,128)(2,1)S(1)} %get-tuple-element.26), channel_id=1, source_target_pairs={{0,8},{4,12},{8,0},{12,4},{16,24},{20,28},{24,16},{28,20},{32,40},... | collective-permute-start | bytes 147464 | tf_op jit(solution)/shard_map/ppermute | solution.py:34
  74.8 9.3 %collective-permute-start.15 = (bf16[64,384]{1,0:T(8,128)(2,1)S(1)}, bf16[64,384]{1,0:T(8,128)(2,1)S(1)}, u32[]{:S(2)}, u32[]{:S(2)}) collective-permute-start(bf16[64,384]{1,0:T(8,128)(2,1)S(1)} %get-tuple-element.27), channel_id=1, source_target_pairs={{0,0},{4,4},{8,16},{12,20},{16,8},{20,12},{24,32},{28,36},{32,24},... | collective-permute-start | bytes 147464 | tf_op jit(solution)/shard_map/ppermute | solution.py:34
